TPU v7x, 32 devices: a whole 2x2x4 slice. The times are simulated.
32 devices in a mesh: ctx: 8 (over z, x), head: 4 (over y, core).
Axes of the slice: x: 2, y: 2, z: 4, core: 2. Of those that a mesh axis runs over, the one named last changes fastest.
Arguments:
- queries: bfloat16 [16384, 128], P(('ctx', 'head')), may hold values from -6 to 6
- keys: bfloat16 [16384, 128], P(('ctx', 'head')), may hold values from -0.0625 to 0.0625
- values: bfloat16 [16384, 4096], P('ctx', 'head'), may hold values from -6 to 6
- tier_weight_rows: int32 [8, 16384], P(None, 'ctx'), may hold values from 0 to 15
- level_table: float32 [16, 32], P(None, 'head'), may hold values from 0.1 to 10
Outputs:
- mixed: bfloat16 [16384, 4096], P('ctx', 'head')
All inputs are finite; a program needn't handle non-finite values.
Results may differ from a plain program's by a relative error of at most 0.0049.
Values may be sent and summed in bfloat16 or wider, within the bound.
No kernel may reach another device: no remote copies, remote signals or barrier semaphores. Data moves between devices by JAX's collectives and lax.ppermute only.
A program may use at most 192 MiB of HBM per device.

v0:
```python
import jax
import jax.numpy as jnp
from jax import lax
from jax.sharding import PartitionSpec as P

GROUP = 128


def swapped(value, axis, distance):
    mask = 2**distance
    pairs = [(source, source ^ mask) for source in range(lax.axis_size(axis))]
    return lax.ppermute(value, axis, pairs)


def local(queries, keys, values, tier_weight_rows, level_table):
    q_whole, k_whole = (
        lax.all_gather(queries, "head", axis=0, tiled=True),
        lax.all_gather(keys, "head", axis=0, tiled=True),
    )
    tok_rows = values.shape[0]
    columns = values.shape[1]
    head_count = level_table.shape[1]
    head_width = columns // head_count
    key_width = q_whole.shape[1]
    local_bits = (tok_rows // GROUP).bit_length() - 1
    context_exponent = lax.axis_size("ctx").bit_length() - 1
    classes = jnp.arange(level_table.shape[0], dtype=jnp.int32)
    onehot = (tier_weight_rows[:, :, None] == classes[None, None, :]).astype(jnp.float32)
    weights = jnp.einsum("ltc,ch->lth", onehot, level_table, precision=lax.Precision.HIGHEST)
    share = weights / jnp.sum(weights, axis=0)
    local_state = lax.dot_general(
        k_whole, values, (((0,), (0,)), ((), ())), preferred_element_type=jnp.float32
    )
    me_index = lax.axis_index("ctx")
    subtree = local_state
    sibling_states = []
    for bit in range(context_exponent):
        incoming_partner_sums = swapped(subtree, "ctx", bit)
        mine_bit = me_index >> bit & 1
        sibling_states.append(
            jnp.where(mine_bit == 1, incoming_partner_sums, jnp.zeros_like(incoming_partner_sums))
        )
        subtree = subtree + incoming_partner_sums

    def weigh(part, level):
        scaled = part.reshape(tok_rows, head_count, head_width) * share[level][:, :, None]
        return scaled.reshape(tok_rows, columns)

    groups = tok_rows // GROUP
    q_groups = q_whole.reshape(groups, GROUP, key_width)
    k_groups = k_whole.reshape(groups, GROUP, key_width)
    scores = jnp.einsum("nik,njk->nij", q_groups, k_groups, preferred_element_type=jnp.float32)
    causal = jnp.tril(jnp.ones((GROUP, GROUP), dtype=bool))
    scores = jnp.where(causal[None], scores, 0.0).astype(jnp.bfloat16)
    near = jnp.einsum(
        "nij,njc->nic",
        scores,
        values.reshape(groups, GROUP, columns),
        preferred_element_type=jnp.float32,
    )
    total = weigh(near.reshape(tok_rows, columns), 0)
    for level in range(1, local_bits + 1):
        half = GROUP * 2 ** (level - 1)
        blocks = tok_rows // (2 * half)
        grouped_probe_matrix = k_whole.reshape(blocks, 2, half, key_width)
        grouped_content_matrix = values.reshape(blocks, 2, half, columns)
        query_blocked = q_whole.reshape(blocks, 2, half, key_width)
        cumulative_memory = jnp.einsum(
            "bsk,bsc->bkc",
            grouped_probe_matrix[:, 0],
            grouped_content_matrix[:, 0],
            preferred_element_type=jnp.float32,
        )
        cumulative_memory = cumulative_memory.astype(jnp.bfloat16)
        upper_half_branch = jnp.einsum(
            "bsk,bkc->bsc",
            query_blocked[:, 1],
            cumulative_memory,
            preferred_element_type=jnp.float32,
        )
        part = jnp.stack([jnp.zeros_like(upper_half_branch), upper_half_branch], axis=1).reshape(
            tok_rows, columns
        )
        total = total + weigh(part, level)
    for bit in range(context_exponent):
        cumulative_memory = sibling_states[bit].astype(jnp.bfloat16)
        part = jnp.dot(q_whole, cumulative_memory, preferred_element_type=jnp.float32)
        total = total + weigh(part, 1 + local_bits + bit)
    return total.astype(jnp.bfloat16)


def solution(mesh):
    placed = (
        P(("ctx", "head"), None),
        P(("ctx", "head"), None),
        P("ctx", "head"),
        P(None, "ctx"),
        P(None, "head"),
    )
    return jax.shard_map(
        local, mesh=mesh, in_specs=placed, out_specs=P("ctx", "head"), check_vma=False
    )
```

profile of v0, /device:TPU:0, one launch (start us, length us, event | category | flops | bytes accessed | tf_op | source)
XLA Modules:
  0.0 162.7 jit_solution(10967841442434719350)
XLA Ops:
  0.0 0.0 copy-start
  0.0 9.0 %all_gather.7 = bf16[2048,128]{1,0:T(8,128)(2,1)S(1)} all-gather(bf16[512,128]{1,0:T(8,128)(2,1)} %param.6), channel_id=1, replica_groups=mesh['ctx'=8,'head'=4] {'head'}, dimensions={0}, use_global_device_ids=true | all-gather | bytes 655360 | tf_op jit(solution)/shard_map/all_gather | solution.py:18
  9.0 2.9 %fusion.36 = f32[128,1024]{1,0:T(8,128)S(1)} fusion(bf16[2048,128]{1,0:T(8,128)(2,1)S(1)} %all_gather.7, bf16[2048,1024]{1,0:T(8,128)(2,1)} %param.7), kind=kOutput, calls=%fused_computation.75 | convolution fusion | flops 536870912 | bytes 5242880 | tf_op jit(solution)/shard_map/dot_general | solution.py:31
  12.0 1.6 collective-permute-start
  13.5 7.2 %all_gather.6 = bf16[2048,128]{1,0:T(8,128)(2,1)S(1)} all-gather(bf16[512,128]{1,0:T(8,128)(2,1)} %param.5), channel_id=1, replica_groups=mesh['ctx'=8,'head'=4] {'head'}, dimensions={0}, use_global_device_ids=true | all-gather | bytes 655360 | tf_op jit(solution)/shard_map/all_gather | solution.py:17
  20.7 0.0 copy-done
  20.7 1.3 fusion.35
  22.1 0.8 slice_bitcast_fusion.51
  22.9 4.7 %convolution_bitcast_fusion.2 = f32[4,1,256,1024]{3,2,1,0:T(8,128)} fusion(bf16[4,2,256,1024]{3,2,1,0:T(8,128)(2,1)} %bitcast.185, bf16[4,2,256,128]{3,2,1,0:T(8,128)(2,1)S(1)} %bitcast.200, bf16[4,2,256,128]{3,2,1,0:T(8,128)(2,1)S(1)} %bitcast.195), kind=kOutput, calls=%fused_computation.18 | convolution fusion | flops 537395200 | bytes 6815744 | tf_op jit(solution)/shard_map/bsk,bkc->bsc/dot_general | solution.py:75
  27.6 4.6 %convolution_bitcast_fusion.1 = f32[2,1,512,1024]{3,2,1,0:T(8,128)} fusion(bf16[2,2,512,1024]{3,2,1,0:T(8,128)(2,1)} %bitcast.186, bf16[2,2,512,128]{3,2,1,0:T(8,128)(2,1)S(1)} %bitcast.201, bf16[2,2,512,128]{3,2,1,0:T(8,128)(2,1)S(1)} %bitcast.196), kind=kOutput, calls=%fused_computation.17 | convolution fusion | flops 537133056 | bytes 6815744 | tf_op jit(solution)/shard_map/bsk,bkc->bsc/dot_general | solution.py:75
  32.2 4.7 %convolution_bitcast_fusion = f32[1,1,1024,1024]{3,2,1,0:T(8,128)} fusion(bf16[1,2,1024,1024]{3,2,1,0:T(8,128)(2,1)} %bitcast.187, bf16[1,2,1024,128]{3,2,1,0:T(8,128)(2,1)S(1)} %bitcast.202, bf16[1,2,1024,128]{3,2,1,0:T(8,128)(2,1)S(1)} %bitcast.197), kind=kOutput, calls=%fused_computation.16 | convolution fusion | flops 537001984 | bytes 6815744 | tf_op jit(solution)/shard_map/bsk,bkc->bsc/dot_general | solution.py:75
  36.9 7.0 %fusion.16 = f32[16,128,1024]{2,1,0:T(8,128)} fusion(bf16[16,128,1024]{2,1,0:T(8,128)(2,1)} %bitcast.188, bf16[16,128,128]{2,1,0:T(8,128)(2,1)S(1)} %bitcast.198, bf16[16,128,128]{2,1,0:T(8,128)(2,1)S(1)} %bitcast.203, pred[128,128]{1,0:T(8,128)(4,1)S(1)} %iota_compare_fusion.2), kind=kOutput, calls=%fused_computation.33 | convolution fusion | flops 604504064 | bytes 13647872 | tf_op jit(solution)/shard_map/nij,njc->nic/dot_general | solution.py:55
  43.9 0.0 collective-permute-done
  43.9 0.1 add.40
  43.9 1.6 %collective-permute-start.1 = (f32[128,1024]{1,0:T(8,128)S(1)}, f32[128,1024]{1,0:T(8,128)S(1)}, u32[]{:S(2)}, u32[]{:S(2)}) collective-permute-start(f32[128,1024]{1,0:T(8,128)S(1)} %add.40), channel_id=1, source_target_pairs={{0,8},{4,12},{8,0},{12,4},{16,24},{20,28},{24,16},{28,20},{1,9},{5... | collective-permute-start | bytes 1572872 | tf_op jit(solution)/shard_map/ppermute | solution.py:12
  45.6 4.9 %convolution_bitcast_fusion.3 = f32[8,1,128,1024]{3,2,1,0:T(8,128)} fusion(bf16[8,2,128,1024]{3,2,1,0:T(8,128)(2,1)} %bitcast.189, bf16[8,2,128,128]{3,2,1,0:T(8,128)(2,1)S(1)} %bitcast.204, bf16[8,2,128,128]{3,2,1,0:T(8,128)(2,1)S(1)} %bitcast.199), kind=kOutput, calls=%fused_computation.19 | convolution fusion | flops 537919488 | bytes 6815744 | tf_op jit(solution)/shard_map/bsk,bkc->bsc/dot_general | solution.py:75
  50.4 6.6 %stack.25.clone = f32[8,2,128,1024]{3,2,1,0:T(8,128)} pad(f32[8,1,128,1024]{3,2,1,0:T(8,128)} %convolution_bitcast_fusion.3, f32[]{:T(128)} %constant.6.clone.1), padding=0_0x1_0x0_0x0_0 | pad | bytes 12582916 | tf_op jit(solution)/shard_map/stack | solution.py:81
  57.0 9.2 %copy.12 = f32[2048,1024]{0,1:T(8,128)} copy(f32[2048,1024]{1,0:T(8,128)} %bitcast.192) | data formatting | bytes 16777216 | tf_op jit(solution)/shard_map/reshape;reshape | solution.py:46
  66.2 6.6 %stack.27.clone = f32[4,2,256,1024]{3,2,1,0:T(8,128)} pad(f32[4,1,256,1024]{3,2,1,0:T(8,128)} %convolution_bitcast_fusion.2, f32[]{:T(128)} %constant.6.clone.1), padding=0_0x1_0x0_0x0_0 | pad | bytes 12582916 | tf_op jit(solution)/shard_map/stack | solution.py:81
  72.8 9.2 %copy.15 = f32[2048,1024]{0,1:T(8,128)} copy(f32[2048,1024]{1,0:T(8,128)} %bitcast.193) | data formatting | bytes 16777216 | tf_op jit(solution)/shard_map/reshape;reshape | solution.py:46
  82.0 6.6 %stack.29.clone = f32[2,2,512,1024]{3,2,1,0:T(8,128)} pad(f32[2,1,512,1024]{3,2,1,0:T(8,128)} %convolution_bitcast_fusion.1, f32[]{:T(128)} %constant.6.clone.1), padding=0_0x1_0x0_0x0_0 | pad | bytes 12582916 | tf_op jit(solution)/shard_map/stack | solution.py:81
  88.5 9.2 %copy.18 = f32[2048,1024]{0,1:T(8,128)} copy(f32[2048,1024]{1,0:T(8,128)} %bitcast.194) | data formatting | bytes 16777216 | tf_op jit(solution)/shard_map/reshape;reshape | solution.py:46
  97.7 6.5 %stack.31 = f32[1,2,1024,1024]{3,2,1,0:T(8,128)} pad(f32[1,1,1024,1024]{3,2,1,0:T(8,128)} %convolution_bitcast_fusion, f32[]{:T(128)} %constant.6.clone.1), padding=0_0x1_0x0_0x0_0 | pad | bytes 12582916 | tf_op jit(solution)/shard_map/stack | solution.py:81
  104.3 9.2 %copy.19 = f32[2048,1024]{0,1:T(8,128)} copy(f32[2048,1024]{1,0:T(8,128)} %bitcast.191) | data formatting | bytes 16777216 | tf_op jit(solution)/shard_map/reshape;reshape | solution.py:46
  113.5 9.2 %copy.9 = f32[2048,1024]{0,1:T(8,128)} copy(f32[2048,1024]{1,0:T(8,128)} %bitcast.190) | data formatting | bytes 16777216 | tf_op jit(solution)/shard_map/reshape;reshape | solution.py:46
  122.7 1.3 fusion.22
  124.0 0.0 collective-permute-done.1
  124.0 0.1 add.42
  124.1 2.6 %collective-permute-start.2 = (bf16[128,1024]{1,0:T(8,128)(2,1)S(1)}, bf16[128,1024]{1,0:T(8,128)(2,1)}, u32[]{:S(2)}, u32[]{:S(2)}) collective-permute-start(bf16[128,1024]{1,0:T(8,128)(2,1)S(1)} %add.42), channel_id=1, source_target_pairs={{0,16},{4,20},{8,24},{12,28},{16,0},{20,4},{24,8},{28,12},{1,17},{... | collective-permute-start | bytes 786440 | tf_op jit(solution)/shard_map/ppermute | solution.py:12
  126.7 1.3 fusion.23
  128.0 10.9 %collective-permute-done.2 = bf16[128,1024]{1,0:T(8,128)(2,1)} collective-permute-done((bf16[128,1024]{1,0:T(8,128)(2,1)S(1)}, bf16[128,1024]{1,0:T(8,128)(2,1)}, u32[]{:S(2)}, u32[]{:S(2)}) %collective-permute-start.2) | collective-permute-done | bytes 262176 | tf_op jit(solution)/shard_map/ppermute | solution.py:12
  139.0 0.0 copy-start.1
  139.0 17.3 %fusion.1 = bf16[2048,1024]{0,1:T(8,128)(2,1)} fusion(f32[1024,2048]{1,0:T(8,128)S(1)} %fusion.23, f32[1024,2048]{1,0:T(8,128)S(1)} %fusion.22, f32[2048,1024]{0,1:T(8,128)} %copy.19, f32[2048,1024]{0,1:T(8,128)} %copy.18, f32[2048,1024]{0,1:T(8,128)} %copy.15, f32[2048,1024]{0,1:T(8,128)} %copy.12, f32[2048,1024]{0,1:T(8,128)} %copy.9, ...), kind=kOutput, calls=%fused_computation.2 | convolution fusion | flops 570556416 | bytes 64225280 | tf_op jit(solution)/shard_map/dot_general | solution.py:87
  156.3 6.4 %copy.20 = bf16[2048,1024]{1,0:T(8,128)(2,1)} copy(bf16[2048,1024]{0,1:T(8,128)(2,1)} %fusion.1) | data formatting | bytes 8388608 | tf_op jit(solution)/shard_map/convert_element_type | solution.py:89
  162.7 0.0 copy-done.1
  (2 shorter events, 0.1 us)
Async XLA Ops:
  0.0 20.7 %copy-start = (f32[16,8]{0,1:T(8,128)S(1)}, f32[16,8]{0,1:T(8,128)}, u32[]{:S(2)}) copy-start(f32[16,8]{0,1:T(8,128)} %param.9) | copy-start | bytes 1540
  12.0 31.9 %collective-permute-start = (f32[128,1024]{1,0:T(8,128)S(1)}, f32[128,1024]{1,0:T(8,128)S(1)}, u32[]{:S(2)}, u32[]{:S(2)}) collective-permute-start(f32[128,1024]{1,0:T(8,128)S(1)} %fusion.36), channel_id=1, source_target_pairs={{0,4},{4,0},{8,12},{12,8},{16,20},{20,16},{24,28},{28,24},{1,5},{5... | collective-permute-start | bytes 1572872 | tf_op jit(solution)/shard_map/ppermute | solution.py:12
  43.9 80.1 %collective-permute-start.1 = (f32[128,1024]{1,0:T(8,128)S(1)}, f32[128,1024]{1,0:T(8,128)S(1)}, u32[]{:S(2)}, u32[]{:S(2)}) collective-permute-start(f32[128,1024]{1,0:T(8,128)S(1)} %add.40), channel_id=1, source_target_pairs={{0,8},{4,12},{8,0},{12,4},{16,24},{20,28},{24,16},{28,20},{1,9},{5... | collective-permute-start | bytes 1572872 | tf_op jit(solution)/shard_map/ppermute | solution.py:12
  124.1 14.9 %collective-permute-start.2 = (bf16[128,1024]{1,0:T(8,128)(2,1)S(1)}, bf16[128,1024]{1,0:T(8,128)(2,1)}, u32[]{:S(2)}, u32[]{:S(2)}) collective-permute-start(bf16[128,1024]{1,0:T(8,128)(2,1)S(1)} %add.42), channel_id=1, source_target_pairs={{0,16},{4,20},{8,24},{12,28},{16,0},{20,4},{24,8},{28,12},{1,17},{... | collective-permute-start | bytes 786440 | tf_op jit(solution)/shard_map/ppermute | solution.py:12
  139.0 23.7 %copy-start.1 = (f32[16,8]{0,1:T(8,128)S(1)}, f32[16,8]{0,1:T(8,128)}, u32[]{:S(2)}) copy-start(f32[16,8]{0,1:T(8,128)} %param.9) | copy-start | bytes 1540
where the time goes:
time: 164 us; the launch traced here: 163 us
  local copies, waits for them, and re-layouts  79.5 us (48%)
  matrix products  49.9 us (30%)
  blocking collectives  16.2 us (10%)
  waiting for transfers between devices  10.9 us (7%)
  starting transfers between devices  5.84 us (4%)
    another operation x5, local copies, waits for them, and re-layouts, weigh(): part.reshape(tok_rows, head_count, head_width) * share[level][:, :, None]  46.1 us
    another operation x4, local copies, waits for them, and re-layouts, local(): jnp.stack([jnp.zeros_like(upper_half_branch), upper_half_branch], axis=1)  26.2 us
    dot_general x3, matrix products, local(): jnp.dot(q_whole, cumulative_memory, preferred_element_type=jnp.float32)  19.9 us
    dot_general x4, matrix products, local(): jnp.einsum('bsk,bkc->bsc', query_blocked[:, 1], cumulative_memory, prefer...  18.8 us
    ppermute x3, waiting for transfers between devices, swapped(): return lax.ppermute(value, axis, pairs)  10.9 us
    all_gather x1, blocking collectives, local(): lax.all_gather(keys, 'head', axis=0, tiled=True)  9 us
    all_gather x1, blocking collectives, local(): lax.all_gather(queries, 'head', axis=0, tiled=True)  7.22 us
    dot_general x1, matrix products, local(): jnp.einsum('nij,njc->nic', scores, values.reshape(groups, GROUP, columns)...  6.98 us
  transfers between devices with their start and end apart: 3, of which 1 were waited for; matrix products, arithmetic and copies ran while one was open for 63% of the time, Pallas kernels for 0%

commit v1 on v0

--- a/solution.py
+++ b/solution.py
@@ -4,6 +4,19 @@
 from jax.sharding import PartitionSpec as P
 
 GROUP = 128
+
+
+def ring_gather(value, axis, dim):
+    ways = lax.axis_size(axis)
+    up = [(d, (d + 1) % ways) for d in range(ways)]
+    down = [(d, (d - 1) % ways) for d in range(ways)]
+    earlier, later = ([value], [value])
+    for _ in range(ways // 2):
+        earlier.append(lax.ppermute(earlier[-1], axis, up))
+    for _ in range((ways - 1) // 2):
+        later.append(lax.ppermute(later[-1], axis, down))
+    line = jnp.concatenate([*earlier[::-1], *later[1:]], axis=dim)
+    return jnp.roll(line, (lax.axis_index(axis) - ways // 2) * value.shape[dim], axis=dim)
 
 
 def swapped(value, axis, distance):
@@ -14,7 +27,7 @@
 
 def local(queries, keys, values, tier_weight_rows, level_table):
     q_whole, k_whole = (
-        lax.all_gather(queries, "head", axis=0, tiled=True),
+        ring_gather(queries, "head", 0),
         lax.all_gather(keys, "head", axis=0, tiled=True),
     )
     tok_rows = values.shape[0]

time: 164 us -> 196 us (1.20)
  matrix products: 49.9 us -> 85.6 us
  blocking collectives: 16.2 us -> 9.07 us
  other arithmetic: 0.19 us -> 3.47 us
  starting transfers between devices: 5.84 us -> 8.33 us
  waiting for transfers between devices: 10.9 us -> 8.44 us
    mul x1 -> x17, local copies, waits for them, and re-layouts: 0.84 us -> 61.4 us  [weigh(): part.reshape(tok_rows, head_count, head_width) * share[level][:, :, None]]
    another operation x5 -> x0, local copies, waits for them, and re-layouts: 46.1 us -> none  [weigh(): part.reshape(tok_rows, head_count, head_width) * share[level][:, :, None]]
    dot_general x3, matrix products: 19.9 us -> 54.7 us  [local(): jnp.dot(q_whole, cumulative_memory, preferred_element_type=jnp.float32)]
    all_gather x1 -> x0, blocking collectives: 7.22 us -> none  [local(): lax.all_gather(queries, 'head', axis=0, tiled=True)]
    another operation x4, local copies, waits for them, and re-layouts: 26.2 us -> 19 us  [local(): jnp.stack([jnp.zeros_like(upper_half_branch), upper_half_branch], axis=1)]
    convert_element_type x1 -> x0, local copies, waits for them, and re-layouts: 6.4 us -> none  [local(): return total.astype(jnp.bfloat16)]
    add x2, other arithmetic: 0.13 us -> 3.41 us  [local(): subtree = subtree + incoming_partner_sums]
    ppermute x0 -> x3, starting transfers between devices: none -> 2.62 us  [the longest x1 2 us: ring_gather(): later.append(lax.ppermute(later[-1], axis, down))]
  transfers between devices with their start and end apart: 3 -> 6, of which waited for: 1 -> 1; matrix products, arithmetic and copies ran while one was open for 63% -> 35% of each run, Pallas kernels for 0% -> 0%
where the time goes in v1:
time: 196 us
  matrix products  85.6 us (44%)
  local copies, waits for them, and re-layouts  80.7 us (41%)
  blocking collectives  9.07 us (5%)
  waiting for transfers between devices  8.44 us (4%)
  starting transfers between devices  8.33 us (4%)
  other arithmetic  3.47 us (2%)
    mul x17, local copies, waits for them, and re-layouts, weigh(): part.reshape(tok_rows, head_count, head_width) * share[level][:, :, None]  61.4 us
    dot_general x3, matrix products, local(): jnp.dot(q_whole, cumulative_memory, preferred_element_type=jnp.float32)  54.7 us
    another operation x4, local copies, waits for them, and re-layouts, local(): jnp.stack([jnp.zeros_like(upper_half_branch), upper_half_branch], axis=1)  19 us
    dot_general x4, matrix products, local(): jnp.einsum('bsk,bkc->bsc', query_blocked[:, 1], cumulative_memory, prefer...  18.8 us
    all_gather x1, blocking collectives, local(): lax.all_gather(keys, 'head', axis=0, tiled=True)  9.07 us
    ppermute x3, waiting for transfers between devices, swapped(): return lax.ppermute(value, axis, pairs)  8.43 us
    dot_general x1, matrix products, local(): jnp.einsum('nij,njc->nic', scores, values.reshape(groups, GROUP, columns)...  7.01 us
    ppermute x3, starting transfers between devices, swapped(): return lax.ppermute(value, axis, pairs)  5.71 us
  transfers between devices with their start and end apart: 6, of which 1 were waited for; matrix products, arithmetic and copies ran while one was open for 35% of the time, Pallas kernels for 0%

profile of v1, /device:TPU:0, one launch (start us, length us, event | category | flops | bytes accessed | tf_op | source)
XLA Modules:
  0.0 195.9 jit_solution(16772380776208880471)
XLA Ops:
  0.0 0.0 copy-start
  0.0 0.5 collective-permute-start
  0.5 2.0 %collective-permute-start.2 = (bf16[512,128]{1,0:T(8,128)(2,1)}, bf16[512,128]{1,0:T(8,128)(2,1)S(1)}, u32[]{:S(2)}, u32[]{:S(2)}) collective-permute-start(bf16[512,128]{1,0:T(8,128)(2,1)} %param.5), channel_id=1, source_target_pairs={{0,3},{1,0},{2,1},{3,2},{4,7},{5,4},{6,5},{7,6},{8,11},{9,8},{10,9... | collective-permute-start | bytes 393224 | tf_op jit(solution)/shard_map/ppermute | solution.py:17
  2.5 9.1 %all_gather.3 = bf16[2048,128]{1,0:T(8,128)(2,1)S(1)} all-gather(bf16[512,128]{1,0:T(8,128)(2,1)} %param.6), channel_id=1, replica_groups=mesh['ctx'=8,'head'=4] {'head'}, dimensions={0}, use_global_device_ids=true | all-gather | bytes 655360 | tf_op jit(solution)/shard_map/all_gather | solution.py:31
  11.6 0.0 copy-start.11
  11.6 3.8 %fusion.36 = f32[128,1024]{1,0:T(8,128)} fusion(bf16[2048,128]{1,0:T(8,128)(2,1)S(1)} %all_gather.3, bf16[2048,1024]{1,0:T(8,128)(2,1)} %param.7), kind=kOutput, calls=%fused_computation.84 | convolution fusion | flops 536870912 | bytes 5242880 | tf_op jit(solution)/shard_map/dot_general | solution.py:44
  15.4 1.5 collective-permute-start.3
  16.8 0.0 copy-done
  16.9 1.3 fusion.35
  18.2 0.0 collective-permute-done
  18.2 0.1 collective-permute-start.1
  18.3 0.7 slice_bitcast_fusion.51
  19.0 0.3 copy.14
  19.3 1.2 copy.27
  20.5 1.3 copy.26
  21.8 1.4 copy.25
  23.2 1.3 copy.24
  24.5 1.3 copy.23
  25.8 1.4 copy.20
  27.2 1.4 copy.17
  28.6 0.0 collective-permute-done.1
  28.7 0.0 copy-done.11
  28.7 0.0 collective-permute-done.2
  28.9 4.6 %convolution_bitcast_fusion.2 = f32[4,1,256,1024]{3,2,1,0:T(8,128)} fusion(bf16[4,2,256,1024]{3,2,1,0:T(8,128)(2,1)} %bitcast.198, bf16[4,2,256,128]{3,2,1,0:T(8,128)(2,1)S(1)} %bitcast.216, bf16[4,2,256,128]{3,2,1,0:T(8,128)(2,1)S(1)} %bitcast.203), kind=kOutput, calls=%fused_computation.18 | convolution fusion | flops 537395200 | bytes 6815744 | tf_op jit(solution)/shard_map/bsk,bkc->bsc/dot_general | solution.py:88
  33.5 4.6 %convolution_bitcast_fusion.1 = f32[2,1,512,1024]{3,2,1,0:T(8,128)} fusion(bf16[2,2,512,1024]{3,2,1,0:T(8,128)(2,1)} %bitcast.199, bf16[2,2,512,128]{3,2,1,0:T(8,128)(2,1)S(1)} %bitcast.217, bf16[2,2,512,128]{3,2,1,0:T(8,128)(2,1)S(1)} %bitcast.204), kind=kOutput, calls=%fused_computation.17 | convolution fusion | flops 537133056 | bytes 6815744 | tf_op jit(solution)/shard_map/bsk,bkc->bsc/dot_general | solution.py:88
  38.1 4.7 %convolution_bitcast_fusion = f32[1,1,1024,1024]{3,2,1,0:T(8,128)} fusion(bf16[1,2,1024,1024]{3,2,1,0:T(8,128)(2,1)} %bitcast.200, bf16[1,2,1024,128]{3,2,1,0:T(8,128)(2,1)S(1)} %bitcast.218, bf16[1,2,1024,128]{3,2,1,0:T(8,128)(2,1)S(1)} %bitcast.205), kind=kOutput, calls=%fused_computation.16 | convolution fusion | flops 537001984 | bytes 6815744 | tf_op jit(solution)/shard_map/bsk,bkc->bsc/dot_general | solution.py:88
  42.8 7.0 %fusion.16 = f32[16,128,1024]{2,1,0:T(8,128)} fusion(bf16[16,128,1024]{2,1,0:T(8,128)(2,1)} %bitcast.201, bf16[16,128,128]{2,1,0:T(8,128)(2,1)S(1)} %bitcast.206, bf16[16,128,128]{2,1,0:T(8,128)(2,1)S(1)} %bitcast.219, pred[128,128]{1,0:T(8,128)(4,1)S(1)} %iota_compare_fusion.2), kind=kOutput, calls=%fused_computation.33 | convolution fusion | flops 604504064 | bytes 13647872 | tf_op jit(solution)/shard_map/nij,njc->nic/dot_general | solution.py:68
  49.8 0.0 collective-permute-done.3
  49.8 2.1 %add.53 = f32[128,1024]{1,0:T(8,128)} add(f32[128,1024]{1,0:T(8,128)} %fusion.36, f32[128,1024]{1,0:T(8,128)} %collective-permute-done.3) | non-fusion elementwise | flops 131072 | bytes 1572864 | tf_op jit(solution)/shard_map/add | solution.py:56
  51.9 1.6 collective-permute-start.4
  53.5 4.9 %convolution_bitcast_fusion.3 = f32[8,1,128,1024]{3,2,1,0:T(8,128)} fusion(bf16[8,2,128,1024]{3,2,1,0:T(8,128)(2,1)} %bitcast.202, bf16[8,2,128,128]{3,2,1,0:T(8,128)(2,1)S(1)} %bitcast.220, bf16[8,2,128,128]{3,2,1,0:T(8,128)(2,1)S(1)} %bitcast.207), kind=kOutput, calls=%fused_computation.19 | convolution fusion | flops 537919488 | bytes 6815744 | tf_op jit(solution)/shard_map/bsk,bkc->bsc/dot_general | solution.py:88
  58.3 0.0 copy-start.4
  58.3 6.7 %stack.25.clone = f32[8,2,128,1024]{3,2,1,0:T(8,128)} pad(f32[8,1,128,1024]{3,2,1,0:T(8,128)} %convolution_bitcast_fusion.3, f32[]{:T(128)} %constant.45.clone.1), padding=0_0x1_0x0_0x0_0 | pad | bytes 12582916 | tf_op jit(solution)/shard_map/stack | solution.py:94
  65.1 0.0 copy-done.4
  65.1 0.0 copy-start.3
  65.1 4.1 %stack.27.clone = f32[4,2,256,1024]{3,2,1,0:T(8,128)} pad(f32[4,1,256,1024]{3,2,1,0:T(8,128)S(1)} %copy-done.4, f32[]{:T(128)} %constant.45.clone.1), padding=0_0x1_0x0_0x0_0 | pad | bytes 12582916 | tf_op jit(solution)/shard_map/stack | solution.py:94
  69.2 0.0 copy-done.3
  69.2 0.0 copy-start.2
  69.2 4.1 %stack.29.clone = f32[2,2,512,1024]{3,2,1,0:T(8,128)} pad(f32[2,1,512,1024]{3,2,1,0:T(8,128)S(1)} %copy-done.3, f32[]{:T(128)} %constant.45.clone.1), padding=0_0x1_0x0_0x0_0 | pad | bytes 12582916 | tf_op jit(solution)/shard_map/stack | solution.py:94
  73.3 0.0 copy-done.2
  73.3 4.1 %stack.31 = f32[1,2,1024,1024]{3,2,1,0:T(8,128)} pad(f32[1,1,1024,1024]{3,2,1,0:T(8,128)S(1)} %copy-done.2, f32[]{:T(128)} %constant.45.clone.1), padding=0_0x1_0x0_0x0_0 | pad | bytes 12582916 | tf_op jit(solution)/shard_map/stack | solution.py:94
  77.4 4.5 %fusion.22 = f32[2048,1024]{1,0:T(8,128)} fusion(bf16[2048,128]{1,0:T(8,128)(2,1)S(1)} %constant_dynamic-slice_fusion, f32[128,1024]{1,0:T(8,128)} %collective-permute-done.3, pred[]{:T(512)S(6)} %eq.28), kind=kOutput, calls=%fused_computation.43 | convolution fusion | flops 537001984 | bytes 9437185 | tf_op jit(solution)/shard_map/dot_general | solution.py:100
  81.9 0.0 copy-start.10
  81.9 0.0 collective-permute-done.4
  81.9 1.3 add.55
  83.2 2.7 %collective-permute-start.5 = (bf16[128,1024]{1,0:T(8,128)(2,1)S(1)}, bf16[128,1024]{1,0:T(8,128)(2,1)S(1)}, u32[]{:S(2)}, u32[]{:S(2)}) collective-permute-start(bf16[128,1024]{1,0:T(8,128)(2,1)S(1)} %add.55), channel_id=1, source_target_pairs={{0,16},{4,20},{8,24},{12,28},{16,0},{20,4},{24,8},{28,12},{1,17},{... | collective-permute-start | bytes 786440 | tf_op jit(solution)/shard_map/ppermute | solution.py:25
  85.9 4.5 %fusion.23 = f32[2048,1024]{1,0:T(8,128)} fusion(bf16[2048,128]{1,0:T(8,128)(2,1)S(1)} %constant_dynamic-slice_fusion, f32[128,1024]{1,0:T(8,128)} %collective-permute-done.4, pred[]{:T(512)S(6)} %eq.29), kind=kOutput, calls=%fused_computation.44 | convolution fusion | flops 537001984 | bytes 9437185 | tf_op jit(solution)/shard_map/dot_general | solution.py:100
  90.3 8.4 %collective-permute-done.5 = bf16[128,1024]{1,0:T(8,128)(2,1)S(1)} collective-permute-done((bf16[128,1024]{1,0:T(8,128)(2,1)S(1)}, bf16[128,1024]{1,0:T(8,128)(2,1)S(1)}, u32[]{:S(2)}, u32[]{:S(2)}) %collective-permute-start.5) | collective-permute-done | bytes 262176 | tf_op jit(solution)/shard_map/ppermute | solution.py:25
  98.8 0.0 copy-done.10
  98.8 6.4 %mul.113 = f32[2048,8,128]{2,1,0:T(8,128)} broadcast(f32[2048,8]{1,0:T(8,128)S(1)} %copy-done.10), dimensions={0,1} | broadcast | bytes 8454144 | tf_op jit(solution)/shard_map/mul | solution.py:59
  105.1 0.0 copy-done.9
  105.1 6.4 %mul.117 = f32[2048,8,128]{2,1,0:T(8,128)} broadcast(f32[2048,8]{1,0:T(8,128)S(1)} %copy-done.9), dimensions={0,1} | broadcast | bytes 8454144 | tf_op jit(solution)/shard_map/mul | solution.py:59
  111.5 0.0 copy-done.8
  111.5 6.5 %mul.121 = f32[2048,8,128]{2,1,0:T(8,128)} broadcast(f32[2048,8]{1,0:T(8,128)S(1)} %copy-done.8), dimensions={0,1} | broadcast | bytes 8454144 | tf_op jit(solution)/shard_map/mul | solution.py:59
  118.0 0.0 copy-done.7
  118.0 6.4 %mul.125 = f32[2048,8,128]{2,1,0:T(8,128)} broadcast(f32[2048,8]{1,0:T(8,128)S(1)} %copy-done.7), dimensions={0,1} | broadcast | bytes 8454144 | tf_op jit(solution)/shard_map/mul | solution.py:59
  124.4 0.0 copy-done.6
  124.4 6.5 %mul.129 = f32[2048,8,128]{2,1,0:T(8,128)} broadcast(f32[2048,8]{1,0:T(8,128)S(1)} %copy-done.6), dimensions={0,1} | broadcast | bytes 8454144 | tf_op jit(solution)/shard_map/mul | solution.py:59
  130.9 0.0 copy-done.5
  130.9 6.3 %mul.133 = f32[2048,8,128]{2,1,0:T(8,128)} broadcast(f32[2048,8]{1,0:T(8,128)S(1)} %copy-done.5), dimensions={0,1} | broadcast | bytes 8454144 | tf_op jit(solution)/shard_map/mul | solution.py:59
  137.3 6.3 %mul.137 = f32[2048,8,128]{2,1,0:T(8,128)} broadcast(f32[2048,8]{1,0:T(8,128)S(1)} %copy.27), dimensions={0,1} | broadcast | bytes 8454144 | tf_op jit(solution)/shard_map/mul | solution.py:59
  143.6 6.3 %mul.109 = f32[2048,8,128]{2,1,0:T(8,128)} broadcast(f32[2048,8]{1,0:T(8,128)S(1)} %copy.14), dimensions={0,1} | broadcast | bytes 8454144 | tf_op jit(solution)/shard_map/mul | solution.py:59
  149.9 45.8 %fusion.1 = bf16[2048,1024]{1,0:T(8,128)(2,1)} fusion(f32[256,8,8,128]{3,2,1,0:T(8,128)} %bitcast.214, f32[2048,1024]{1,0:T(8,128)} %fusion.23, f32[256,8,8,128]{3,2,1,0:T(8,128)} %bitcast.213, f32[2048,1024]{1,0:T(8,128)} %fusion.22, f32[256,8,8,128]{3,2,1,0:T(8,128)} %bitcast.212, f32[256,8,8,128]{3,2,1,0:T(8,128)} %bitcast.211, ...), kind=kOutput, calls=%fused_computation.2 | convolution fusion | flops 570556416 | bytes 130809856 | tf_op jit(solution)/shard_map/dot_general | solution.py:100
  195.7 0.0 copy-done.1
  (17 shorter events, 0.3 us)
Async XLA Ops:
  0.0 16.9 %copy-start = (f32[16,8]{0,1:T(8,128)S(1)}, f32[16,8]{0,1:T(8,128)}, u32[]{:S(2)}) copy-start(f32[16,8]{0,1:T(8,128)} %param.9) | copy-start | bytes 1540
  0.0 18.2 %collective-permute-start = (bf16[512,128]{1,0:T(8,128)(2,1)}, bf16[512,128]{1,0:T(8,128)(2,1)S(1)}, u32[]{:S(2)}, u32[]{:S(2)}) collective-permute-start(bf16[512,128]{1,0:T(8,128)(2,1)} %param.5), channel_id=1, source_target_pairs={{0,1},{1,2},{2,3},{3,0},{4,5},{5,6},{6,7},{7,4},{8,9},{9,10},{10,1... | collective-permute-start | bytes 393224 | tf_op jit(solution)/shard_map/ppermute | solution.py:15
  0.5 28.2 %collective-permute-start.2 = (bf16[512,128]{1,0:T(8,128)(2,1)}, bf16[512,128]{1,0:T(8,128)(2,1)S(1)}, u32[]{:S(2)}, u32[]{:S(2)}) collective-permute-start(bf16[512,128]{1,0:T(8,128)(2,1)} %param.5), channel_id=1, source_target_pairs={{0,3},{1,0},{2,1},{3,2},{4,7},{5,4},{6,5},{7,6},{8,11},{9,8},{10,9... | collective-permute-start | bytes 393224 | tf_op jit(solution)/shard_map/ppermute | solution.py:17
  11.6 17.1 %copy-start.11 = (bf16[512,128]{1,0:T(8,128)(2,1)S(1)}, bf16[512,128]{1,0:T(8,128)(2,1)}, u32[]{:S(2)}) copy-start(bf16[512,128]{1,0:T(8,128)(2,1)} %param.5) | copy-start | bytes 393220
  15.4 34.5 %collective-permute-start.3 = (f32[128,1024]{1,0:T(8,128)}, f32[128,1024]{1,0:T(8,128)}, u32[]{:S(2)}, u32[]{:S(2)}) collective-permute-start(f32[128,1024]{1,0:T(8,128)} %fusion.36), channel_id=1, source_target_pairs={{0,4},{4,0},{8,12},{12,8},{16,20},{20,16},{24,28},{28,24},{1,5},{5... | collective-permute-start | bytes 1572872 | tf_op jit(solution)/shard_map/ppermute | solution.py:25
  18.2 10.4 %collective-permute-start.1 = (bf16[512,128]{1,0:T(8,128)(2,1)S(1)}, bf16[512,128]{1,0:T(8,128)(2,1)S(1)}, u32[]{:S(2)}, u32[]{:S(2)}) collective-permute-start(bf16[512,128]{1,0:T(8,128)(2,1)S(1)} %collective-permute-done), channel_id=1, source_target_pairs={{0,1},{1,2},{2,3},{3,0},{4,5},{5,6},{6,7},{7,4},{8,9},{9,10},{10,1... | collective-permute-start | bytes 393224 | tf_op jit(solution)/shard_map/ppermute | solution.py:15
  51.9 30.0 %collective-permute-start.4 = (f32[128,1024]{1,0:T(8,128)}, f32[128,1024]{1,0:T(8,128)}, u32[]{:S(2)}, u32[]{:S(2)}) collective-permute-start(f32[128,1024]{1,0:T(8,128)} %add.53), channel_id=1, source_target_pairs={{0,8},{4,12},{8,0},{12,4},{16,24},{20,28},{24,16},{28,20},{1,9},{5... | collective-permute-start | bytes 1572872 | tf_op jit(solution)/shard_map/ppermute | solution.py:25
  58.3 6.7 %copy-start.4 = (f32[4,1,256,1024]{3,2,1,0:T(8,128)S(1)}, f32[4,1,256,1024]{3,2,1,0:T(8,128)}, u32[]{:S(2)}) copy-start(f32[4,1,256,1024]{3,2,1,0:T(8,128)} %convolution_bitcast_fusion.2) | copy-start | bytes 12582916
  65.1 4.1 %copy-start.3 = (f32[2,1,512,1024]{3,2,1,0:T(8,128)S(1)}, f32[2,1,512,1024]{3,2,1,0:T(8,128)}, u32[]{:S(2)}) copy-start(f32[2,1,512,1024]{3,2,1,0:T(8,128)} %convolution_bitcast_fusion.1) | copy-start | bytes 12582916
  69.2 4.1 %copy-start.2 = (f32[1,1,1024,1024]{3,2,1,0:T(8,128)S(1)}, f32[1,1,1024,1024]{3,2,1,0:T(8,128)}, u32[]{:S(2)}) copy-start(f32[1,1,1024,1024]{3,2,1,0:T(8,128)} %convolution_bitcast_fusion) | copy-start | bytes 12582916
  81.9 16.9 %copy-start.10 = (f32[2048,8]{1,0:T(8,128)S(1)}, f32[2048,8]{1,0:T(8,128)}, u32[]{:S(2)}) copy-start(f32[2048,8]{1,0:T(8,128)} %copy.17) | copy-start | bytes 196612
  83.2 15.6 %collective-permute-start.5 = (bf16[128,1024]{1,0:T(8,128)(2,1)S(1)}, bf16[128,1024]{1,0:T(8,128)(2,1)S(1)}, u32[]{:S(2)}, u32[]{:S(2)}) collective-permute-start(bf16[128,1024]{1,0:T(8,128)(2,1)S(1)} %add.55), channel_id=1, source_target_pairs={{0,16},{4,20},{8,24},{12,28},{16,0},{20,4},{24,8},{28,12},{1,17},{... | collective-permute-start | bytes 786440 | tf_op jit(solution)/shard_map/ppermute | solution.py:25
  90.3 14.8 %copy-start.9 = (f32[2048,8]{1,0:T(8,128)S(1)}, f32[2048,8]{1,0:T(8,128)}, u32[]{:S(2)}) copy-start(f32[2048,8]{1,0:T(8,128)} %copy.20) | copy-start | bytes 196612
  90.3 21.2 %copy-start.8 = (f32[2048,8]{1,0:T(8,128)S(1)}, f32[2048,8]{1,0:T(8,128)}, u32[]{:S(2)}) copy-start(f32[2048,8]{1,0:T(8,128)} %copy.23) | copy-start | bytes 196612
  105.1 12.9 %copy-start.7 = (f32[2048,8]{1,0:T(8,128)S(1)}, f32[2048,8]{1,0:T(8,128)}, u32[]{:S(2)}) copy-start(f32[2048,8]{1,0:T(8,128)} %copy.24) | copy-start | bytes 196612
  111.5 12.9 %copy-start.6 = (f32[2048,8]{1,0:T(8,128)S(1)}, f32[2048,8]{1,0:T(8,128)}, u32[]{:S(2)}) copy-start(f32[2048,8]{1,0:T(8,128)} %copy.25) | copy-start | bytes 196612
  118.0 12.9 %copy-start.5 = (f32[2048,8]{1,0:T(8,128)S(1)}, f32[2048,8]{1,0:T(8,128)}, u32[]{:S(2)}) copy-start(f32[2048,8]{1,0:T(8,128)} %copy.26) | copy-start | bytes 196612
  149.9 45.8 %copy-start.1 = (f32[16,8]{0,1:T(8,128)S(1)}, f32[16,8]{0,1:T(8,128)}, u32[]{:S(2)}) copy-start(f32[16,8]{0,1:T(8,128)} %param.9) | copy-start | bytes 1540
